TPU v7x, 512 devices: a whole 4x8x8 slice. The times are simulated.
512 devices in a mesh: feat: 128 (over y, x, z_lo, core), layer: 4 (over z_hi).
Axes of the slice: x: 4, y: 8, z: 8 (z_hi: 4, z_lo: 2; z = z_hi * 2 + z_lo), core: 2. Of those that a mesh axis runs over, the one named last changes fastest.
Arguments:
- residual_in: bfloat16 [4, 384, 2304], P('layer', 'feat'), as said below
- enc_weight: bfloat16 [4, 2304, 8192], P('layer', None, 'feat'), as said below
- thresholds: int32 [4, 8192], P('layer', 'feat'), may hold values from -2016 to 7341, as said below
- dec_weight: bfloat16 [4, 4, 8192, 2304], P(None, 'layer', 'feat'), may hold values from -0.03125 to 0.03125
- target: bfloat16 [4, 384, 2304], P('layer', 'feat')
Outputs:
- loss_value: float32 [], replicated
- reconstruction: bfloat16 [4, 384, 2304], P('layer', 'feat')
- dec_grad: bfloat16 [4, 4, 8192, 2304], P(None, 'layer', 'feat')
- enc_grad: bfloat16 [4, 2304, 8192], P('layer', None, 'feat')
Inputs may be any that keep to these rules, and one draw needn't show every extreme that they name: `residual_in`: every entry is a multiple of 1/8. `enc_weight`: every entry is a multiple of 1/256. `thresholds`: whole numbers.
All inputs are finite; a program needn't handle non-finite values.
Results may differ from a plain program's by a relative error of at most 0.007.
Values may be sent and summed in bfloat16 or wider, within the bound.
A program may use at most 64 MiB of HBM per device.

v0:
```python
import jax
import jax.numpy as jnp
from jax import lax
from jax.sharding import PartitionSpec as P

ERROR_SCALE = 32.0
PENALTY_WEIGHT = 4.0


def body(residual_in, enc_weight, thresholds, dec_weight, target):
    local_rows = residual_in[0]
    encoder = enc_weight[0]
    jump_level = (thresholds[0].astype(jnp.float32) + 0.5) / 2048.0
    preactivation = jnp.dot(
        lax.all_gather(local_rows, "feat", axis=0, tiled=True),
        encoder,
        preferred_element_type=jnp.float32,
    )
    active_mask = preactivation > jump_level[None, :]
    layer_activations = jnp.where(active_mask, preactivation, 0.0).astype(jnp.bfloat16)
    token_count = preactivation.shape[0]
    magnitude = jnp.mean(jnp.abs(layer_activations.astype(jnp.float32)), axis=0)
    penalty_local = jnp.sum(magnitude * magnitude)
    penalty_total = lax.psum(penalty_local, ("feat", "layer"))
    all_acts = lax.all_gather(layer_activations[None], "layer", axis=0, tiled=True)
    decoder = dec_weight[:, 0]
    recon = lax.psum_scatter(
        jnp.einsum("sif,sfd->id", all_acts, decoder, preferred_element_type=jnp.float32),
        "feat",
        scatter_dimension=0,
        tiled=True,
    )
    error_rows = recon - target[0].astype(jnp.float32)
    grad_local = (error_rows / ERROR_SCALE).astype(jnp.bfloat16)
    grad_all = lax.all_gather(grad_local, "feat", axis=0, tiled=True)
    squares_local = jnp.sum(error_rows * error_rows)
    squares_total = lax.psum(squares_local, ("feat", "layer"))
    dec_grad = jnp.einsum(
        "sif,id->sfd", all_acts, grad_all, preferred_element_type=jnp.float32
    ).astype(jnp.bfloat16)
    act_part = jnp.einsum("id,sfd->sif", grad_all, decoder, preferred_element_type=jnp.float32)
    activation_gradient = lax.psum_scatter(act_part, "layer", scatter_dimension=0, tiled=True)[0]
    sparsity_gradient = (
        2.0
        * PENALTY_WEIGHT
        * magnitude[None, :]
        * jnp.sign(layer_activations.astype(jnp.float32))
        / token_count
    )
    preactivation_gradient = jnp.where(
        active_mask, activation_gradient + sparsity_gradient, 0.0
    ).astype(jnp.bfloat16)
    enc_grad = jnp.einsum(
        "id,if->df",
        lax.all_gather(local_rows, "feat", axis=0, tiled=True),
        preactivation_gradient,
        preferred_element_type=jnp.float32,
    )
    loss_value = (squares_total + 2.0 * ERROR_SCALE * PENALTY_WEIGHT * penalty_total) / (
        lax.axis_size("layer") * token_count * local_rows.shape[1]
    )
    return (
        loss_value,
        recon.astype(jnp.bfloat16)[None],
        dec_grad[:, None],
        enc_grad.astype(jnp.bfloat16)[None],
    )


def solution(mesh):
    return jax.shard_map(
        body,
        mesh=mesh,
        in_specs=(
            P("layer", "feat", None),
            P("layer", None, "feat"),
            P("layer", "feat"),
            P(None, "layer", "feat", None),
            P("layer", "feat", None),
        ),
        out_specs=(
            P(),
            P("layer", "feat", None),
            P(None, "layer", "feat", None),
            P("layer", None, "feat"),
        ),
        check_vma=False,
    )
```

profile of v0, /device:TPU:1, one launch (start us, length us, event | category | flops | bytes accessed | tf_op | source)
XLA Modules:
  0.0 1679.2 jit_solution(8954540019723485133)
XLA Ops:
  7.2 0.0 copy-start
  7.2 0.0 all-gather.6.cloned.1.call-start
  7.2 1.4 copy.19
  8.7 0.0 all-gather.6.cloned.1.call-update
  8.7 0.0 all-reduce.4.cloned.1.call-start
  8.7 0.7 multiply_bitcast_fusion
  9.4 223.4 %all-gather.6.cloned.1.call-done = bf16[1,384,2304]{2,0,1:T(2,128)(2,1)} async-done(((bf16[1,3,2304]{2,0,1:T(2,128)(2,1)}), bf16[1,384,2304]{2,0,1:T(2,128)(2,1)}) %all-gather.6.cloned.1.call-update) | async-done | bytes 1769488 | tf_op jit(solution)/shard_map/all_gather | solution.py:15
  232.8 2.8 fusion.14
  235.6 14.4 all-gather.1
  250.1 0.0 copy-done
  250.1 2.5 convolution_bitcast_fusion
  252.6 0.0 copy-start.1
  252.6 0.0 all-reduce.4.cloned.1.call-update
  252.6 0.0 all-gather.8.cloned.1.call-start
  252.6 1.3 dynamic-slice
  254.6 1085.1 %all-reduce.4.cloned.1.call-done = f32[384,2304]{1,0:T(8,128)} async-done(((f32[384,2304]{1,0:T(8,128)}), f32[384,2304]{1,0:T(8,128)}) %all-reduce.4.cloned.1.call-update) | async-done | bytes 3538960
  1339.7 0.0 copy-done.1
  1339.7 2.1 fusion.26
  1341.8 0.0 all-gather.8.cloned.1.call-update
  1341.8 0.0 reduce-scatter.2.cloned.1.call-start
  1341.9 215.0 %all-gather.8.cloned.1.call-done = bf16[128,3,2304]{2,1,0:T(4,128)(2,1)} async-done(((bf16[1,3,2304]{2,1,0:T(4,128)(2,1)}), bf16[128,3,2304]{2,1,0:T(4,128)(2,1)}) %all-gather.8.cloned.1.call-update) | async-done | bytes 1769488 | tf_op jit(solution)/shard_map/all_gather | solution.py:35
  1556.9 4.1 reshape.20
  1561.0 1.6 convolution_bitcast_fusion.1
  1562.5 0.0 reduce-scatter.2.cloned.1.call-update
  1562.5 0.6 broadcast_multiply_fusion
  1563.2 100.5 %all-reduce.1 = (f32[]{:T(128)}, f32[]{:T(128)}) all-reduce(f32[]{:T(128)} %get-tuple-element.25, f32[]{:T(128)} %get-tuple-element.27), channel_id=1, replica_groups=mesh['feat'=128,'layer'=4] {'feat','layer'}, use_global_device_ids=true, to_apply=%region_2.3 | all-reduce | flops 2 | bytes 16 | tf_op jit(solution)/shard_map/psum | solution.py:37
  1664.9 1.5 fusion.25
  1666.5 1.8 fusion
  1668.3 0.0 reduce-scatter.2.cloned.1.call-done
  1668.3 3.3 fusion.1
Async XLA Ops:
  7.2 242.9 %copy-start = (bf16[4,1,64,2304]{3,2,1,0:T(8,128)(2,1)S(1)}, bf16[4,1,64,2304]{3,2,1,0:T(8,128)(2,1)}, u32[]{:S(2)}) copy-start(bf16[4,1,64,2304]{3,2,1,0:T(8,128)(2,1)} %param.8) | copy-start | bytes 3538948
  7.2 225.6 %all-gather.6.cloned.1.call-start = ((), (), s32[]{:S(2)}) async-start(), calls=%async_computation.2 | async-start | bytes 3566592 | tf_op jit(solution)/shard_map/all_gather | solution.py:15
  8.7 1331.0 %all-reduce.4.cloned.1.call-start = ((), (), s32[]{:S(2)}) async-start(), calls=%async_computation.4 | async-start | bytes 7077888
  252.6 1087.1 %copy-start.1 = (bf16[1,3,2304]{2,1,0:T(4,128)(2,1)S(1)}, bf16[1,3,2304]{2,1,0:T(4,128)(2,1)}, u32[]{:S(2)}) copy-start(bf16[1,3,2304]{2,1,0:T(4,128)(2,1)} %param.9) | copy-start | bytes 41476
  252.6 1304.3 %all-gather.8.cloned.1.call-start = ((), (), s32[]{:S(2)}) async-start(), calls=%async_computation.3 | async-start | bytes 2377728 | tf_op jit(solution)/shard_map/all_gather | solution.py:35
  1341.8 326.4 %reduce-scatter.2.cloned.1.call-start = ((), (), s32[]{:S(2)}) async-start(), calls=%async_computation.1 | async-start | bytes 491520 | tf_op jit(solution)/shard_map/reduce_scatter | solution.py:42
Sparse Core Ops, SparseCore 0:
  10.7 222.0 all-gather.5
  252.7 1086.9 all-reduce.3
  1342.4 214.4 all-gather.7
  1562.7 29.0 reduce-scatter.1
where the time goes:
time: 1680 us
  waiting for transfers between devices  1520 us (90%)
  blocking collectives  115 us (7%)
  between operations  16.9 us (1%)
    unnamed x5, waiting for transfers between devices  1090 us
    all_gather x1, waiting for transfers between devices, body(): lax.all_gather(local_rows, 'feat', axis=0, tiled=True)  223 us
    all_gather x1, waiting for transfers between devices, body(): grad_all = lax.all_gather(grad_local, 'feat', axis=0, tiled=True)  215 us
    psum x1, blocking collectives, body(): squares_total = lax.psum(squares_local, ('feat', 'layer'))  100 us
  transfers between devices with their start and end apart: 4, of which 3 were waited for; matrix products, arithmetic and copies ran while one was open for 0% of the time, Pallas kernels for 0%

commit v1 on v0

v1 whole, which is shorter than its diff:
```python
import functools

import jax
import jax.numpy as jnp
from jax import lax
from jax.experimental import pallas as pl
from jax.experimental.pallas import tpu as pltpu
from jax.sharding import PartitionSpec as P

ERROR_SCALE = 32.0
PENALTY_WEIGHT = 4.0
MESH = pl.DeviceIdType.MESH
PLANE = 8
CORES = 2
NCH = 6
BF = jnp.bfloat16
F32 = jnp.float32


def nt(a, b):
    return lax.dot_general(a, b, (((1,), (1,)), ((), ())), preferred_element_type=F32)


def nn(a, b):
    return lax.dot_general(a, b, (((1,), (0,)), ((), ())), preferred_element_type=F32)


def kernel(
    dims,
    x_in, enc_in, th_in, dec_in, tgt_in,
    loss_out, rec_out, dg_out, eg_out,
    st, gs, gown, tmp, xb, gb, xp, gp,
    encb, decb, cutb, msum, pre, acts, act_t, act_o,
    part, rs_s, rs_r, so, si,
    agf, ags, agr, pgt, pgo, dgv, egv,
    sc_p, sc_y, sc_l, sc_c,
    loc_sem, d2d_s, d2d_r, pl_s, pl_r, ring_s, ring_r, lay_s, lay_r, ys_s, ys_r,
):
    ny, nl, r, d, f = dims
    half = ny // 2
    cw = d // NCH
    rows = PLANE * r
    tokens = ny * rows * CORES
    feat = lax.axis_index("feat")
    zh = lax.axis_index("layer")
    c = lax.rem(feat, CORES)
    p = lax.rem(feat // CORES, PLANE)
    y = feat // (CORES * PLANE)

    def dev(yy, pp, cc, ll):
        return (yy * (PLANE * CORES) + pp * CORES + cc, ll)

    def ymod(v):
        return lax.rem(v + 2 * ny, ny)

    def pmod(v):
        return lax.rem(v + PLANE, PLANE)

    def lmod(v):
        return lax.rem(v + nl, nl)

    def remote(src, dst, ss, rs, device):
        return pltpu.make_async_remote_copy(
            src_ref=src, dst_ref=dst, send_sem=ss, recv_sem=rs, device_id=device, device_id_type=MESH
        )

    partner = dev(y, p, 1 - c, zh)

    enc_cp = pltpu.make_async_copy(enc_in, encb.at[c], loc_sem.at[0])
    enc_cp.start()
    dec_cp = pltpu.make_async_copy(dec_in, decb.at[:, c], loc_sem.at[1])
    dec_cp.start()
    x_cp = pltpu.make_async_copy(x_in, st.at[p], loc_sem.at[2])
    x_cp.start()

    cut = (th_in[...].astype(F32) + 0.5) / 2048.0
    zero = jnp.zeros_like(cut)
    cutb[0] = jnp.where(c == 0, jnp.concatenate([cut, zero], 1), jnp.concatenate([zero, cut], 1))

    barrier = pltpu.get_barrier_semaphore()
    peers = [dev(y, pmod(p + j), c, zh) for j in range(1, PLANE)]
    peers += [dev(ymod(y + j), p, c, zh) for j in range(1, ny)]
    peers += [dev(y, p, c, lmod(zh + j)) for j in range(1, nl)]
    peers += [partner]
    for peer in peers:
        pl.semaphore_signal(barrier, inc=1, device_id=peer, device_id_type=MESH)
    pl.semaphore_wait(barrier, len(peers))

    pending = []

    def plane_start(which, source, dest):
        out = []
        for j in range(1, PLANE):
            q = pmod(p + j)
            cp = remote(source(q), dest.at[p], pl_s.at[which, j - 1], pl_r.at[which, j - 1], dev(y, q, c, zh))
            cp.start()
            out.append(cp)
        pending.extend(out)
        return out

    def d2d_start(which, source, dest):
        cp = remote(source, dest, d2d_s.at[which], d2d_r.at[which], partner)
        cp.start()
        pending.append(cp)
        return cp

    def repack(staged, block):
        for i in range(PLANE):
            tmp[r * i : r * (i + 1), :] = staged[i].astype(F32)
        block[y] = tmp[...].astype(BF)

    def ring_copy(base, buf, way, s, k):
        blk = ymod(y - s) if way == 0 else ymod(y + s)
        to = ymod(y + 1) if way == 0 else ymod(y - 1)
        piece = buf.at[blk, :, pl.ds(k * cw, cw)]
        return remote(piece, piece, ring_s.at[base, way, s, k], ring_r.at[base, way, s, k], dev(to, p, c, zh))

    def lanes(way, s):
        if s < half - 1:
            return range(NCH)
        return range(NCH // 2) if way == 0 else range(NCH // 2, NCH)

    def ring_gather(base, buf):
        sent = []
        for k in range(NCH):
            for way in (0, 1):
                if k in lanes(way, 0):
                    cp = ring_copy(base, buf, way, 0, k)
                    cp.start()
                    sent.append(cp)
        for s in range(half):
            for k in range(NCH):
                for way in (0, 1):
                    if k in lanes(way, s):
                        ring_copy(base, buf, way, s, k).wait_recv()
                        if s + 1 < half and k in lanes(way, s + 1):
                            cp = ring_copy(base, buf, way, s + 1, k)
                            cp.start()
                            sent.append(cp)
        pending.extend(sent)

    xs = plane_start(0, lambda q: x_in, st)
    enc_d = d2d_start(0, enc_in, encb.at[c])
    cut_d = d2d_start(2, cutb.at[0], cutb.at[1])
    dec_d = d2d_start(1, dec_in, decb.at[:, c])
    x_cp.wait()
    for cp in xs:
        cp.wait_recv()
    repack(st, xb)
    ring_gather(0, xb)
    x_d = d2d_start(4, xb, xp)

    enc_cp.wait()
    enc_d.wait_recv()
    cut_d.wait_recv()
    xv = xb[...].reshape(ny * rows, d)
    ev = encb[...].reshape(CORES * f, d)
    pa = nt(xv, ev)
    pre[...] = pa
    level = cutb[0] + cutb[1]
    act = jnp.where(pa > level, pa, 0.0).astype(BF)
    acts[zh] = act

    def layer_start(which, source, dest):
        out = []
        for j in range(1, nl):
            l = lmod(zh + j)
            cp = remote(source(l), dest.at[zh], lay_s.at[which, j - 1], lay_r.at[which, j - 1], dev(y, p, c, l))
            cp.start()
            out.append(cp)
        pending.extend(out)
        return out

    al = layer_start(0, lambda l: acts.at[zh], acts)
    msum[0] = jnp.sum(jnp.abs(act.astype(F32)), axis=0, keepdims=True)
    mag_d = d2d_start(3, msum.at[0], msum.at[1])
    dec_cp.wait()
    dec_d.wait_recv()
    for cp in al:
        cp.wait_recv()

    av = jnp.concatenate([acts[s] for s in range(nl)], axis=1)
    part[...] = nn(av, decb[...].reshape(nl * CORES * f, d)).reshape(ny, rows, d)

    def rs_lanes(way, s):
        return lanes(way, half - 1 - s)

    def rs_copy(way, s, k):
        to = ymod(y + 1) if way == 0 else ymod(y - 1)
        cols = pl.ds(k * cw, cw)
        return remote(
            rs_s.at[way, s, :, cols], rs_r.at[way, s, :, cols],
            ring_s.at[2, way, s, k], ring_r.at[2, way, s, k], dev(to, p, c, zh),
        )

    def rs_step(way, s, k):
        blk = ymod(y + half - s) if way == 0 else ymod(y - half + s)
        cols = pl.ds(k * cw, cw)
        value = part[blk, :, cols]
        if s > 0 and k in rs_lanes(way, s - 1):
            rs_copy(way, s - 1, k).wait_recv()
            value = value + rs_r[way, s - 1, :, cols].astype(F32)
        rs_s[way, s, :, cols] = value.astype(BF)
        cp = rs_copy(way, s, k)
        cp.start()
        pending.append(cp)

    for s in range(half):
        for k in range(NCH):
            for way in (0, 1):
                if k in rs_lanes(way, s):
                    rs_step(way, s, k)

    for s in range(nl):
        act_t[s] = jnp.transpose(acts[s].astype(F32)).astype(BF)
    act_d = d2d_start(5, act_t.at[:, pl.ds(pl.multiple_of((1 - c) * f, f), f)], act_o)

    for k in range(NCH):
        cols = pl.ds(k * cw, cw)
        for way in (0, 1):
            rs_copy(way, half - 1, k).wait_recv()
        tmp[:, cols] = part[y, :, cols] + rs_r[0, half - 1, :, cols].astype(F32) + rs_r[1, half - 1, :, cols].astype(F32)
    for i in range(PLANE):
        so[i] = tmp[r * i : r * (i + 1), :].astype(BF)
    ps = plane_start(1, lambda q: so.at[q], si)
    si[p] = so[p]
    for cp in ps:
        cp.wait_recv()
    recon = si[0].astype(F32)
    for i in range(1, PLANE):
        recon = recon + si[i].astype(F32)
    rec_out[...] = recon.astype(BF)
    error = recon - tgt_in[...].astype(F32)
    gown[...] = (error * (1.0 / ERROR_SCALE)).astype(BF)
    gs[p] = gown[...]
    gsd = plane_start(2, lambda q: gown, gs)
    mag_d.wait_recv()
    magnitude = (msum[0] + msum[1]) * (1.0 / tokens)
    penalty = jnp.sum(magnitude * magnitude)
    scalar = jnp.sum(error * error) + (2.0 * ERROR_SCALE * PENALTY_WEIGHT / CORES) * penalty
    sc_p[p] = jnp.full((1, 128), scalar, F32)
    scp = plane_start(3, lambda q: sc_p.at[p], sc_p)
    for cp in gsd:
        cp.wait_recv()
    repack(gs, gb)
    ring_gather(1, gb)
    g_d = d2d_start(6, gb, gp)

    gv = gb[...].reshape(ny * rows, d)
    for s in range(nl):
        ag = nt(gv, decb[s].reshape(CORES * f, d))
        agf[s] = ag
        ags[s] = ag.astype(BF)
    agl = layer_start(1, lambda l: ags.at[l], agr)

    def fold(slots, n):
        total = slots[0]
        for i in range(1, n):
            total = total + slots[i]
        return total

    for cp in scp:
        cp.wait_recv()
    sc_y[y] = fold(sc_p, PLANE)
    scy = []
    for j in range(1, ny):
        to = ymod(y + j)
        cp = remote(sc_y.at[y], sc_y.at[y], ys_s.at[j - 1], ys_r.at[j - 1], dev(to, p, c, zh))
        cp.start()
        scy.append(cp)
    pending.extend(scy)

    act_d.wait_recv()
    g_d.wait_recv()
    go = gp[...].reshape(ny * rows, d)
    own = pl.ds(pl.multiple_of(c * f, f), f)
    lhs = jnp.concatenate([act_t[s, own, :] for s in range(nl)], axis=0)
    lho = jnp.concatenate([act_o[s] for s in range(nl)], axis=0)
    dgv[...] = (nn(lhs, gv) + nn(lho, go)).astype(BF).reshape(nl, f, d)
    dg_cp = pltpu.make_async_copy(dgv, dg_out, loc_sem.at[3])
    dg_cp.start()

    for cp in scy:
        cp.wait_recv()
    sc_l[zh] = fold(sc_y, ny)
    scl = layer_start(2, lambda l: sc_l.at[zh], sc_l)

    for cp in agl:
        cp.wait_recv()
    act_grad = agf[zh]
    for j in range(1, nl):
        act_grad = act_grad + agr[lmod(zh + j)].astype(F32)
    pv = pre[...]
    fire = pv > level
    sign = jnp.where(fire & (pv > 0.0), 1.0, 0.0) - jnp.where(fire & (pv < 0.0), 1.0, 0.0)
    sparsity = (2.0 * PENALTY_WEIGHT) * magnitude * sign / float(tokens)
    pg = jnp.where(fire, act_grad + sparsity, 0.0)
    pgt[...] = jnp.transpose(pg).astype(BF)
    pg_d = d2d_start(7, pgt.at[pl.ds(pl.multiple_of((1 - c) * f, f), f)], pgo)
    for cp in scl:
        cp.wait_recv()
    sc_c[c] = fold(sc_l, nl)
    sc_d = d2d_start(8, sc_c.at[c], sc_c.at[c])
    x_d.wait_recv()
    eg = nn(pgt[own, :], xb[...].reshape(ny * rows, d))
    pg_d.wait_recv()
    eg = eg + nn(pgo[...], xp[...].reshape(ny * rows, d))
    egv[...] = eg.astype(BF)
    eg_cp = pltpu.make_async_copy(egv, eg_out, loc_sem.at[4])
    eg_cp.start()
    sc_d.wait_recv()
    loss_out[...] = fold(sc_c, CORES) * (1.0 / (nl * tokens * d))
    for cp in pending:
        cp.wait_send()
    dg_cp.wait()
    eg_cp.wait()


def solution(mesh):
    nl = mesh.shape["layer"]
    ny = mesh.shape["feat"] // (PLANE * CORES)

    def body(residual_in, enc_weight, thresholds, dec_weight, target):
        r, d = residual_in.shape[1:]
        f = enc_weight.shape[2]
        rows = PLANE * r
        half = ny // 2
        t = ny * rows
        any_spec = pl.BlockSpec(memory_space=pl.ANY)
        vm = pl.BlockSpec(memory_space=pltpu.VMEM)
        V = pltpu.VMEM
        dma = pltpu.SemaphoreType.DMA
        loss, rec, dg, eg = pl.pallas_call(
            functools.partial(kernel, (ny, nl, r, d, f)),
            out_shape=(
                jax.ShapeDtypeStruct((1, 128), F32),
                jax.ShapeDtypeStruct((r, d), BF),
                jax.ShapeDtypeStruct((nl, f, d), BF),
                jax.ShapeDtypeStruct((f, d), BF),
            ),
            in_specs=[any_spec, any_spec, vm, any_spec, vm],
            out_specs=(vm, vm, any_spec, any_spec),
            scratch_shapes=[
                V((PLANE, r, d), BF), V((PLANE, r, d), BF), V((r, d), BF), V((rows, d), F32),
                V((ny, rows, d), BF), V((ny, rows, d), BF), V((ny, rows, d), BF), V((ny, rows, d), BF),
                V((CORES, f, d), BF), V((nl, CORES, f, d), BF), V((2, 1, CORES * f), F32), V((2, 1, CORES * f), F32),
                V((t, CORES * f), F32), V((nl, t, CORES * f), BF), V((nl, CORES * f, t), BF), V((nl, f, t), BF),
                V((ny, rows, d), F32), V((2, half, rows, d), BF), V((2, half, rows, d), BF),
                V((PLANE, r, d), BF), V((PLANE, r, d), BF),
                V((nl, t, CORES * f), F32), V((nl, t, CORES * f), BF), V((nl, t, CORES * f), BF),
                V((CORES * f, t), BF), V((f, t), BF), V((nl, f, d), BF), V((f, d), BF),
                V((PLANE, 1, 128), F32), V((ny, 1, 128), F32), V((nl, 1, 128), F32), V((CORES, 1, 128), F32),
                dma((5,)), dma((9,)), dma((9,)), dma((4, PLANE - 1)), dma((4, PLANE - 1)),
                dma((3, 2, half, NCH)), dma((3, 2, half, NCH)), dma((3, nl - 1)), dma((3, nl - 1)),
                dma((ny - 1,)), dma((ny - 1,)),
            ],
            compiler_params=pltpu.CompilerParams(
                collective_id=0, has_side_effects=True, vmem_limit_bytes=56 * 1024 * 1024
            ),
            name="step",
        )(
            residual_in[0],
            jnp.swapaxes(enc_weight[0], 0, 1),
            thresholds,
            dec_weight[:, 0],
            target[0],
        )
        return loss[0, 0], rec[None], dg[:, None], jnp.swapaxes(eg, 0, 1)[None]

    return jax.shard_map(
        body,
        mesh=mesh,
        in_specs=(
            P("layer", "feat", None),
            P("layer", None, "feat"),
            P("layer", "feat"),
            P(None, "layer", "feat", None),
            P("layer", "feat", None),
        ),
        out_specs=(
            P(),
            P("layer", "feat", None),
            P(None, "layer", "feat", None),
            P("layer", None, "feat"),
        ),
        check_vma=False,
    )
```

time: 1680 us -> 102 us (0.06)
  waiting for transfers between devices: 1520 us -> 0 us
  blocking collectives: 115 us -> 0 us
  Pallas kernels: 0 us -> 94.7 us
    unnamed x5 -> x0, waiting for transfers between devices: 1090 us -> none
    all_gather x2 -> x0, waiting for transfers between devices: 438 us -> none  [the longest x1 223 us: body(): lax.all_gather(local_rows, 'feat', axis=0, tiled=True)]
    psum x1 -> x0, blocking collectives: 100 us -> none  [body(): squares_total = lax.psum(squares_local, ('feat', 'layer'))]
    pallas_call x0 -> x1, Pallas kernels: none -> 94.7 us  [body(): pl.pallas_call(functools.partial(kernel, (ny, nl, r, d, f)), out_shape=(j...]
  transfers between devices with their start and end apart: 4 -> 0, of which waited for: 3 -> 0; matrix products, arithmetic and copies ran while one was open for 0% -> 0% of each run, Pallas kernels for 0% -> 0%
where the time goes in v1:
time: 102 us; the launch traced here: 101 us
  Pallas kernels  94.7 us (93%)
  local copies, waits for them, and re-layouts  4.46 us (4%)
  between operations  2.33 us (2%)
    pallas_call x1, Pallas kernels, body(): pl.pallas_call(functools.partial(kernel, (ny, nl, r, d, f)), out_shape=(j...  94.7 us
    unnamed x5, local copies, waits for them, and re-layouts  4.46 us

profile of v1, /device:TPU:1, one launch (start us, length us, event | category | flops | bytes accessed | tf_op | source)
XLA Modules:
  0.0 101.5 jit_solution(8922517215893729243)
XLA Ops:
  0.6 94.7 %step.1 = (f32[1,128]{1,0:T(1,128)}, bf16[3,2304]{1,0:T(4,128)(2,1)}, bf16[4,64,2304]{2,1,0:T(8,128)(2,1)}, bf16[64,2304]{1,0:T(8,128)(2,1)}) custom-call(bf16[3,2304]{1,0:T(4,128)(2,1)} %bitcast.20, bf16[64,2304]{1,0:T(8,128)(2,1)} %bitcast.18, s32[1,64]{1,0:T(1,128)} %th_in.1, bf16[4,64,2304]{2,1,0:T(8,128)(2,1)} %bitcast.15, bf16[3,2304]{1,0:T(4,128)(2,1)} %bitcast.21), custom_call_target="tpu_custom_call" | custom-call | tf_op jit(solution)/shard_map/step/pallas_call | solution.py:333
  95.9 1.3 %copy.15 = bf16[1,3,2304]{2,1,0:T(4,128)(2,1)} copy(bf16[1,3,2304]{2,1,0:T(4,128)(2,1)} %bitcast.19) | data formatting | bytes 27648
  97.2 0.0 copy-start
  97.2 2.4 %copy.16 = bf16[4,1,64,2304]{3,2,1,0:T(8,128)(2,1)} copy(bf16[4,1,64,2304]{3,2,1,0:T(8,128)(2,1)} %bitcast.16) | data formatting | bytes 2359296
  99.6 0.0 copy-done
  99.6 0.7 copy.17
Async XLA Ops:
  97.2 2.4 %copy-start = (bf16[64,2304]{1,0:T(8,128)(2,1)S(1)}, bf16[64,2304]{1,0:T(8,128)(2,1)}, u32[]{:S(2)}) copy-start(bf16[64,2304]{1,0:T(8,128)(2,1)} %get-tuple-element.11) | copy-start | bytes 884740

commit v2 on v1

v2 whole, which is shorter than its diff:
```python
import functools

import jax
import jax.numpy as jnp
import numpy as np
from jax import lax
from jax.experimental import pallas as pl
from jax.experimental.pallas import tpu as pltpu
from jax.sharding import PartitionSpec as P

ERROR_SCALE = 32.0
PENALTY_WEIGHT = 4.0
MESH = pl.DeviceIdType.MESH
PLANE = 8
CORES = 2
PARTS = 3
BF = jnp.bfloat16
F32 = jnp.float32


def nt(a, b):
    return lax.dot_general(a, b, (((1,), (1,)), ((), ())), preferred_element_type=F32)


def nn(a, b):
    return lax.dot_general(a, b, (((1,), (0,)), ((), ())), preferred_element_type=F32)


def kernel(
    dims,
    x_in, enc_in, th_in, dec_in, tgt_in, perm_in,
    loss_out, rec_out, dg_out, eg_out,
    st_a, st_b, gs_a, gs_b, gown, tmp_a, tmp_b, xb, gb, xp, gp, xq, gq,
    thr, tgt, encb, decb, cutb, msum, pre, acts, act_t, act_o, perm,
    part_a, part_b, rs_a, rs_b, rr_a, rr_b, so_a, so_b, si_a, si_b,
    agf, ags, agr, pgt, pgo,
    sc_p, sc_y, sc_l, sc_c,
    loc_sem, d2d_s, d2d_r, pl_s, pl_r, ys_s, ys_r, lay_s, lay_r,
):
    ny, nl, r, d, f = dims
    wa = d // PARTS
    wb = d - wa
    ca, cb = pl.ds(0, wa), pl.ds(wa, wb)
    rows = PLANE * r
    rows_b = ny * r
    tokens = ny * rows * CORES
    feat = lax.axis_index("feat")
    zh = lax.axis_index("layer")
    c = lax.rem(feat, CORES)
    p = lax.rem(feat // CORES, PLANE)
    y = feat // (CORES * PLANE)

    def dev(yy, pp, cc, ll):
        return (yy * (PLANE * CORES) + pp * CORES + cc, ll)

    def ymod(v):
        return lax.rem(v + 2 * ny, ny)

    def pmod(v):
        return lax.rem(v + PLANE, PLANE)

    def lmod(v):
        return lax.rem(v + nl, nl)

    def remote(src, dst, ss, rs, device):
        return pltpu.make_async_remote_copy(
            src_ref=src, dst_ref=dst, send_sem=ss, recv_sem=rs, device_id=device, device_id_type=MESH
        )

    partner = dev(y, p, 1 - c, zh)

    enc_cp = pltpu.make_async_copy(enc_in, encb.at[c], loc_sem.at[0])
    enc_cp.start()
    dec_cp = pltpu.make_async_copy(dec_in, decb.at[:, c], loc_sem.at[1])
    dec_cp.start()
    xa_cp = pltpu.make_async_copy(x_in.at[:, ca], st_a.at[p], loc_sem.at[2])
    xa_cp.start()
    xb_cp = pltpu.make_async_copy(x_in.at[:, cb], st_b.at[y], loc_sem.at[3])
    xb_cp.start()
    perm_cp = pltpu.make_async_copy(perm_in, perm, loc_sem.at[4])
    perm_cp.start()
    th_cp = pltpu.make_async_copy(th_in, thr, loc_sem.at[5])
    th_cp.start()
    tgt_cp = pltpu.make_async_copy(tgt_in, tgt, loc_sem.at[6])
    tgt_cp.start()
    th_cp.wait()

    cut = (thr[...].astype(F32) + 0.5) / 2048.0
    zero = jnp.zeros_like(cut)
    cutb[0] = jnp.where(c == 0, jnp.concatenate([cut, zero], 1), jnp.concatenate([zero, cut], 1))

    barrier = pltpu.get_barrier_semaphore()
    peers = [dev(y, pmod(p + j), c, zh) for j in range(1, PLANE)]
    peers += [dev(ymod(y + j), p, c, zh) for j in range(1, ny)]
    peers += [dev(y, p, c, lmod(zh + j)) for j in range(1, nl)]
    peers += [partner]
    for peer in peers:
        pl.semaphore_signal(barrier, inc=1, device_id=peer, device_id_type=MESH)
    pl.semaphore_wait(barrier, len(peers))

    pending = []

    def plane_start(which, source, dest):
        out = []
        for j in range(1, PLANE):
            q = pmod(p + j)
            cp = remote(source(q), dest.at[p], pl_s.at[which, j - 1], pl_r.at[which, j - 1], dev(y, q, c, zh))
            cp.start()
            out.append(cp)
        pending.extend(out)
        return out

    def d2d_start(which, source, dest):
        cp = remote(source, dest, d2d_s.at[which], d2d_r.at[which], partner)
        cp.start()
        pending.append(cp)
        return cp

    def y_start(which, source, dest):
        out = []
        for j in range(1, ny):
            q = ymod(y + j)
            cp = remote(source(q), dest.at[y], ys_s.at[which, j - 1], ys_r.at[which, j - 1], dev(q, p, c, zh))
            cp.start()
            out.append(cp)
        pending.extend(out)
        return out

    def wait_all(copies):
        for cp in copies:
            cp.wait_recv()

    def repack(staged, tmp, n):
        for i in range(n):
            tmp[r * i : r * (i + 1), :] = staged[i].astype(F32)
        return tmp[...].astype(BF)

    def gather(which, first_a, first_b, in_a, in_b, buf, quilt):
        wait_all(first_a)
        buf[y, :, ca] = repack(in_a, tmp_a, PLANE)
        last_a = y_start(which + 1, lambda q: buf.at[y, :, ca], buf.at[:, :, ca])
        wait_all(first_b)
        quilt[p] = repack(in_b, tmp_b, ny)
        last_b = plane_start(which + 1, lambda q: quilt.at[p], quilt)
        wait_all(last_b)
        fixed = nn(perm[0], quilt[...].reshape(PLANE * rows_b, wb)).astype(BF)
        buf[:, :, cb] = fixed.reshape(ny, rows, wb)
        wait_all(last_a)

    first_b = y_start(0, lambda q: x_in.at[:, cb], st_b)
    first_a = plane_start(0, lambda q: x_in.at[:, ca], st_a)
    enc_d = d2d_start(0, enc_in, encb.at[c])
    cut_d = d2d_start(2, cutb.at[0], cutb.at[1])
    dec_d = d2d_start(1, dec_in, decb.at[:, c])
    xa_cp.wait()
    xb_cp.wait()
    perm_cp.wait()
    tgt_cp.wait()
    gather(0, first_a, first_b, st_a, st_b, xb, xq)
    x_d = d2d_start(4, xb, xp)

    enc_cp.wait()
    enc_d.wait_recv()
    cut_d.wait_recv()
    xv = xb[...].reshape(ny * rows, d)
    ev = encb[...].reshape(CORES * f, d)
    pa = nt(xv, ev)
    pre[...] = pa
    level = cutb[0] + cutb[1]
    act = jnp.where(pa > level, pa, 0.0).astype(BF)
    acts[zh] = act

    def layer_start(which, source, dest):
        out = []
        for j in range(1, nl):
            l = lmod(zh + j)
            cp = remote(source(l), dest.at[zh], lay_s.at[which, j - 1], lay_r.at[which, j - 1], dev(y, p, c, l))
            cp.start()
            out.append(cp)
        pending.extend(out)
        return out

    al = layer_start(0, lambda l: acts.at[zh], acts)
    msum[0] = jnp.sum(jnp.abs(act.astype(F32)), axis=0, keepdims=True)
    mag_d = d2d_start(3, msum.at[0], msum.at[1])
    dec_cp.wait()
    dec_d.wait_recv()
    for cp in al:
        cp.wait_recv()

    av = jnp.concatenate([acts[s] for s in range(nl)], axis=1)
    qv = nn(perm[1], av).astype(BF)
    dv = decb[...].reshape(nl * CORES * f, d)
    out_b = nn(qv, dv[:, wa:]).reshape(PLANE, rows_b, wb)
    part_b[...] = out_b
    rs_b[...] = out_b.astype(BF)
    down_b = plane_start(2, lambda q: rs_b.at[q], rr_b)
    out_a = nn(av, dv[:, :wa]).reshape(ny, rows, wa)
    part_a[...] = out_a
    rs_a[...] = out_a.astype(BF)
    down_a = y_start(2, lambda q: rs_a.at[q], rr_a)

    for s in range(nl):
        act_t[s] = jnp.transpose(acts[s].astype(F32)).astype(BF)
    act_d = d2d_start(5, act_t.at[:, pl.ds(pl.multiple_of((1 - c) * f, f), f)], act_o)

    wait_all(down_b)
    total = part_b[p]
    for j in range(1, PLANE):
        total = total + rr_b[pmod(p + j)].astype(F32)
    tmp_b[...] = total
    for i in range(ny):
        so_b[i] = tmp_b[r * i : r * (i + 1), :].astype(BF)
    own_b = y_start(3, lambda q: so_b.at[q], si_b)
    si_b[y] = so_b[y]
    wait_all(down_a)
    total = part_a[y]
    for j in range(1, ny):
        total = total + rr_a[ymod(y + j)].astype(F32)
    tmp_a[...] = total
    for i in range(PLANE):
        so_a[i] = tmp_a[r * i : r * (i + 1), :].astype(BF)
    own_a = plane_start(3, lambda q: so_a.at[q], si_a)
    si_a[p] = so_a[p]

    def added(slots, n):
        total = slots[0].astype(F32)
        for i in range(1, n):
            total = total + slots[i].astype(F32)
        return total

    wait_all(own_b)
    recon_b = added(si_b, ny)
    wait_all(own_a)
    recon_a = added(si_a, PLANE)
    recon = jnp.concatenate([recon_a, recon_b], axis=1)
    rec_out[...] = recon.astype(BF)
    error = recon - tgt[...].astype(F32)
    gown[...] = (error * (1.0 / ERROR_SCALE)).astype(BF)
    first_b = y_start(4, lambda q: gown.at[:, cb], gs_b)
    first_a = plane_start(4, lambda q: gown.at[:, ca], gs_a)
    gs_a[p] = gown[:, ca]
    gs_b[y] = gown[:, cb]
    mag_d.wait_recv()
    magnitude = (msum[0] + msum[1]) * (1.0 / tokens)
    penalty = jnp.sum(magnitude * magnitude)
    scalar = jnp.sum(error * error) + (2.0 * ERROR_SCALE * PENALTY_WEIGHT / CORES) * penalty
    sc_p[p] = jnp.full((1, 128), scalar, F32)
    scp = plane_start(6, lambda q: sc_p.at[p], sc_p)
    gather(4, first_a, first_b, gs_a, gs_b, gb, gq)
    g_d = d2d_start(6, gb, gp)

    gv = gb[...].reshape(ny * rows, d)
    agl = []
    for j in range(1, nl):
        l = lmod(zh + j)
        ags[j] = nt(gv, decb[l].reshape(CORES * f, d)).astype(BF)
        cp = remote(ags.at[j], agr.at[zh], lay_s.at[1, j - 1], lay_r.at[1, j - 1], dev(y, p, c, l))
        cp.start()
        agl.append(cp)
    pending.extend(agl)
    agf[...] = nt(gv, decb[zh].reshape(CORES * f, d))

    def fold(slots, n):
        total = slots[0]
        for i in range(1, n):
            total = total + slots[i]
        return total

    for cp in scp:
        cp.wait_recv()
    sc_y[y] = fold(sc_p, PLANE)
    scy = y_start(6, lambda q: sc_y.at[y], sc_y)

    act_d.wait_recv()
    g_d.wait_recv()
    go = gp[...].reshape(ny * rows, d)
    own = pl.ds(pl.multiple_of(c * f, f), f)
    lhs = jnp.concatenate([act_t[s, own, :] for s in range(nl)], axis=0)
    lho = jnp.concatenate([act_o[s] for s in range(nl)], axis=0)
    dg_out[...] = (nn(lhs, gv) + nn(lho, go)).astype(BF).reshape(nl, f, d)

    for cp in scy:
        cp.wait_recv()
    sc_l[zh] = fold(sc_y, ny)
    scl = layer_start(2, lambda l: sc_l.at[zh], sc_l)

    for cp in agl:
        cp.wait_recv()
    act_grad = agf[...]
    for j in range(1, nl):
        act_grad = act_grad + agr[lmod(zh + j)].astype(F32)
    pv = pre[...]
    fire = pv > level
    sign = jnp.where(fire & (pv > 0.0), 1.0, 0.0) - jnp.where(fire & (pv < 0.0), 1.0, 0.0)
    sparsity = (2.0 * PENALTY_WEIGHT) * magnitude * sign / float(tokens)
    pg = jnp.where(fire, act_grad + sparsity, 0.0)
    pgt[...] = jnp.transpose(pg).astype(BF)
    pg_d = d2d_start(7, pgt.at[pl.ds(pl.multiple_of((1 - c) * f, f), f)], pgo)
    for cp in scl:
        cp.wait_recv()
    sc_c[c] = fold(sc_l, nl)
    sc_d = d2d_start(8, sc_c.at[c], sc_c.at[c])
    x_d.wait_recv()
    eg = nn(pgt[own, :], xb[...].reshape(ny * rows, d))
    pg_d.wait_recv()
    eg = eg + nn(pgo[...], xp[...].reshape(ny * rows, d))
    eg_out[...] = eg.astype(BF)
    sc_d.wait_recv()
    loss_out[...] = fold(sc_c, CORES) * (1.0 / (nl * tokens * d))
    for cp in pending:
        cp.wait_send()


def emit(loss_in, rec_in, dg_in, eg_in, loss_out, rec_out, dg_out, eg_out, sem):
    pairs = ((dg_in, dg_out), (eg_in, eg_out), (rec_in, rec_out), (loss_in, loss_out))
    copies = [pltpu.make_async_copy(a, b, sem.at[i]) for i, (a, b) in enumerate(pairs)]
    for cp in copies:
        cp.start()
    for cp in copies:
        cp.wait()


def solution(mesh):
    nl = mesh.shape["layer"]
    ny = mesh.shape["feat"] // (PLANE * CORES)

    def body(residual_in, enc_weight, thresholds, dec_weight, target):
        r, d = residual_in.shape[1:]
        f = enc_weight.shape[2]
        rows = PLANE * r
        wa = d // PARTS
        wb = d - wa
        rows_b = ny * r
        t = ny * rows
        spot = np.arange(t).reshape(PLANE, ny, r).transpose(1, 0, 2).reshape(t)
        eye = np.eye(t, dtype=np.float32)
        perm = jnp.asarray(np.stack([eye[spot], eye[spot].T]), BF)
        any_spec = pl.BlockSpec(memory_space=pl.ANY)
        vm = pl.BlockSpec(memory_space=pltpu.VMEM)
        hbm = pl.BlockSpec(memory_space=pltpu.HBM)
        V = pltpu.VMEM
        dma = pltpu.SemaphoreType.DMA
        shapes = (
            jax.ShapeDtypeStruct((1, 128), F32),
            jax.ShapeDtypeStruct((r, d), BF),
            jax.ShapeDtypeStruct((nl, f, d), BF),
            jax.ShapeDtypeStruct((f, d), BF),
        )
        results = pl.pallas_call(
            functools.partial(kernel, (ny, nl, r, d, f)),
            out_shape=shapes,
            in_specs=[hbm] * 6,
            out_specs=(vm, vm, vm, vm),
            scratch_shapes=[
                V((PLANE, r, wa), BF), V((ny, r, wb), BF), V((PLANE, r, wa), BF), V((ny, r, wb), BF),
                V((r, d), BF), V((rows, wa), F32), V((rows_b, wb), F32),
                V((ny, rows, d), BF), V((ny, rows, d), BF), V((ny, rows, d), BF), V((ny, rows, d), BF),
                V((PLANE, rows_b, wb), BF), V((PLANE, rows_b, wb), BF),
                V((1, f), jnp.int32), V((r, d), BF),
                V((CORES, f, d), BF), V((nl, CORES, f, d), BF), V((2, 1, CORES * f), F32), V((2, 1, CORES * f), F32),
                V((t, CORES * f), F32), V((nl, t, CORES * f), BF), V((nl, CORES * f, t), BF), V((nl, f, t), BF), V((2, t, t), BF),
                V((ny, rows, wa), F32), V((PLANE, rows_b, wb), F32),
                V((ny, rows, wa), BF), V((PLANE, rows_b, wb), BF), V((ny, rows, wa), BF), V((PLANE, rows_b, wb), BF),
                V((PLANE, r, wa), BF), V((ny, r, wb), BF), V((PLANE, r, wa), BF), V((ny, r, wb), BF),
                V((t, CORES * f), F32), V((nl, t, CORES * f), BF), V((nl, t, CORES * f), BF),
                V((CORES * f, t), BF), V((f, t), BF),
                V((PLANE, 1, 128), F32), V((ny, 1, 128), F32), V((nl, 1, 128), F32), V((CORES, 1, 128), F32),
                dma((7,)), dma((9,)), dma((9,)), dma((7, PLANE - 1)), dma((7, PLANE - 1)),
                dma((7, ny - 1)), dma((7, ny - 1)), dma((3, nl - 1)), dma((3, nl - 1)),
            ],
            compiler_params=pltpu.CompilerParams(
                collective_id=0, has_side_effects=True, vmem_limit_bytes=32 * 1024 * 1024
            ),
            name="step",
        )(
            *(
                pltpu.with_memory_space_constraint(v, pltpu.HBM)
                for v in (
                    residual_in[0],
                    jnp.swapaxes(enc_weight[0], 0, 1),
                    thresholds,
                    dec_weight[:, 0],
                    target[0],
                    perm,
                )
            )
        )
        loss, rec, dg, eg = pl.pallas_call(
            emit,
            out_shape=shapes,
            in_specs=[any_spec] * 4,
            out_specs=[hbm] * 4,
            scratch_shapes=[dma((4,))],
            compiler_params=pltpu.CompilerParams(vmem_limit_bytes=1024 * 1024),
            name="emit",
        )(*results)
        return loss[0, 0], rec[None], dg[:, None], jnp.swapaxes(eg, 0, 1)[None]

    return jax.shard_map(
        body,
        mesh=mesh,
        in_specs=(
            P("layer", "feat", None),
            P("layer", None, "feat"),
            P("layer", "feat"),
            P(None, "layer", "feat", None),
            P("layer", "feat", None),
        ),
        out_specs=(
            P(),
            P("layer", "feat", None),
            P(None, "layer", "feat", None),
            P("layer", None, "feat"),
        ),
        check_vma=False,
    )
```

time: 102 us -> 82.9 us (0.81)
  Pallas kernels: 94.7 us -> 82.1 us
  local copies, waits for them, and re-layouts: 4.46 us -> 0 us
  between operations: 2.33 us -> 0.64 us
    pallas_call x1 -> x2, Pallas kernels: 94.7 us -> 82.1 us  [the longest x1 81 us: body(): pl.pallas_call(functools.partial(kernel, (ny, nl, r, d, f)), out_shape=sh...]
    unnamed x5 -> x0, local copies, waits for them, and re-layouts: 4.46 us -> none
where the time goes in v2:
time: 82.9 us; the launch traced here: 82.7 us
  Pallas kernels  82.1 us (99%)
    pallas_call x1, Pallas kernels, body(): pl.pallas_call(functools.partial(kernel, (ny, nl, r, d, f)), out_shape=sh...  81 us

profile of v2, /device:TPU:1, one launch (start us, length us, event | category | flops | bytes accessed | tf_op | source)
XLA Modules:
  0.0 82.7 jit_solution(9781629349989899876)
XLA Ops:
  0.6 81.0 %step.1 = (f32[1,128]{1,0:T(1,128)S(1)}, bf16[3,2304]{1,0:T(4,128)(2,1)S(1)}, bf16[4,64,2304]{2,1,0:T(8,128)(2,1)S(1)}, bf16[64,2304]{1,0:T(8,128)(2,1)S(1)}) custom-call(bf16[3,2304]{1,0:T(4,128)(2,1)} %bitcast.17, bf16[64,2304]{1,0:T(8,128)(2,1)} %bitcast.16, s32[1,64]{1,0:T(1,128)} %th_in.1, bf16[4,64,2304]{2,1,0:T(8,128)(2,1)} %bitcast.15, ...), custom_call_target="tpu_custom_call" | custom-call | tf_op jit(solution)/shard_map/step/pallas_call | solution.py:350
  81.6 1.1 %emit.1 = (f32[1,128]{1,0:T(1,128)}, bf16[3,2304]{1,0:T(4,128)(2,1)}, bf16[4,64,2304]{2,1,0:T(8,128)(2,1)}, bf16[64,2304]{1,0:T(8,128)(2,1)}) custom-call(f32[1,128]{1,0:T(1,128)S(1)} %get-tuple-element.12.loss_in, bf16[3,2304]{1,0:T(4,128)(2,1)S(1)} %get-tuple-element.13.rec_in, bf16[4,64,2304]{2,1,0:T(8,128)(2,1)S(1)} %get-tuple-element.14.dg_in, ...), custom_call_target="tpu_custom_call" | custom-call | tf_op jit(solution)/shard_map/emit/pallas_call | solution.py:389

commit v3 on v2

--- a/solution.py
+++ b/solution.py
@@ -135,13 +135,15 @@
             tmp[r * i : r * (i + 1), :] = staged[i].astype(F32)
         return tmp[...].astype(BF)
 
-    def gather(which, first_a, first_b, in_a, in_b, buf, quilt):
+    def gather(which, first_a, first_b, in_a, in_b, buf, quilt, between=None):
         wait_all(first_a)
         buf[y, :, ca] = repack(in_a, tmp_a, PLANE)
         last_a = y_start(which + 1, lambda q: buf.at[y, :, ca], buf.at[:, :, ca])
         wait_all(first_b)
         quilt[p] = repack(in_b, tmp_b, ny)
         last_b = plane_start(which + 1, lambda q: quilt.at[p], quilt)
+        if between is not None:
+            between()
         wait_all(last_b)
         fixed = nn(perm[0], quilt[...].reshape(PLANE * rows_b, wb)).astype(BF)
         buf[:, :, cb] = fixed.reshape(ny, rows, wb)
@@ -247,7 +249,20 @@
     scalar = jnp.sum(error * error) + (2.0 * ERROR_SCALE * PENALTY_WEIGHT / CORES) * penalty
     sc_p[p] = jnp.full((1, 128), scalar, F32)
     scp = plane_start(6, lambda q: sc_p.at[p], sc_p)
-    gather(4, first_a, first_b, gs_a, gs_b, gb, gq)
+    def fold(slots, n):
+        total = slots[0]
+        for i in range(1, n):
+            total = total + slots[i]
+        return total
+
+    scy = []
+
+    def scalar_y():
+        wait_all(scp)
+        sc_y[y] = fold(sc_p, PLANE)
+        scy.extend(y_start(6, lambda q: sc_y.at[y], sc_y))
+
+    gather(4, first_a, first_b, gs_a, gs_b, gb, gq, scalar_y)
     g_d = d2d_start(6, gb, gp)
 
     gv = gb[...].reshape(ny * rows, d)
@@ -259,18 +274,10 @@
         cp.start()
         agl.append(cp)
     pending.extend(agl)
+    wait_all(scy)
+    sc_l[zh] = fold(sc_y, ny)
+    scl = layer_start(2, lambda l: sc_l.at[zh], sc_l)
     agf[...] = nt(gv, decb[zh].reshape(CORES * f, d))
-
-    def fold(slots, n):
-        total = slots[0]
-        for i in range(1, n):
-            total = total + slots[i]
-        return total
-
-    for cp in scp:
-        cp.wait_recv()
-    sc_y[y] = fold(sc_p, PLANE)
-    scy = y_start(6, lambda q: sc_y.at[y], sc_y)
 
     act_d.wait_recv()
     g_d.wait_recv()
@@ -280,10 +287,10 @@
     lho = jnp.concatenate([act_o[s] for s in range(nl)], axis=0)
     dg_out[...] = (nn(lhs, gv) + nn(lho, go)).astype(BF).reshape(nl, f, d)
 
-    for cp in scy:
+    for cp in scl:
         cp.wait_recv()
-    sc_l[zh] = fold(sc_y, ny)
-    scl = layer_start(2, lambda l: sc_l.at[zh], sc_l)
+    sc_c[c] = fold(sc_l, nl)
+    sc_d = d2d_start(8, sc_c.at[c], sc_c.at[c])
 
     for cp in agl:
         cp.wait_recv()
@@ -297,10 +304,6 @@
     pg = jnp.where(fire, act_grad + sparsity, 0.0)
     pgt[...] = jnp.transpose(pg).astype(BF)
     pg_d = d2d_start(7, pgt.at[pl.ds(pl.multiple_of((1 - c) * f, f), f)], pgo)
-    for cp in scl:
-        cp.wait_recv()
-    sc_c[c] = fold(sc_l, nl)
-    sc_d = d2d_start(8, sc_c.at[c], sc_c.at[c])
     x_d.wait_recv()
     eg = nn(pgt[own, :], xb[...].reshape(ny * rows, d))
     pg_d.wait_recv()

time: 82.9 us -> 77.9 us (0.940)
  Pallas kernels: 82.1 us -> 77.1 us
    pallas_call x1, Pallas kernels: 81 us -> 76 us  [body(): pl.pallas_call(functools.partial(kernel, (ny, nl, r, d, f)), out_shape=sh...]
where the time goes in v3:
time: 77.9 us; the launch traced here: 77.7 us
  Pallas kernels  77.1 us (99%)
    pallas_call x1, Pallas kernels, body(): pl.pallas_call(functools.partial(kernel, (ny, nl, r, d, f)), out_shape=sh...  76 us

profile of v3, /device:TPU:1, one launch (start us, length us, event | category | flops | bytes accessed | tf_op | source)
XLA Modules:
  0.0 77.7 jit_solution(14435866028698807002)
XLA Ops:
  0.6 76.0 %step.1 = (f32[1,128]{1,0:T(1,128)S(1)}, bf16[3,2304]{1,0:T(4,128)(2,1)S(1)}, bf16[4,64,2304]{2,1,0:T(8,128)(2,1)S(1)}, bf16[64,2304]{1,0:T(8,128)(2,1)S(1)}) custom-call(bf16[3,2304]{1,0:T(4,128)(2,1)} %bitcast.17, bf16[64,2304]{1,0:T(8,128)(2,1)} %bitcast.16, s32[1,64]{1,0:T(1,128)} %th_in.1, bf16[4,64,2304]{2,1,0:T(8,128)(2,1)} %bitcast.15, ...), custom_call_target="tpu_custom_call" | custom-call | tf_op jit(solution)/shard_map/step/pallas_call | solution.py:353
  76.6 1.1 %emit.1 = (f32[1,128]{1,0:T(1,128)}, bf16[3,2304]{1,0:T(4,128)(2,1)}, bf16[4,64,2304]{2,1,0:T(8,128)(2,1)}, bf16[64,2304]{1,0:T(8,128)(2,1)}) custom-call(f32[1,128]{1,0:T(1,128)S(1)} %get-tuple-element.12.loss_in, bf16[3,2304]{1,0:T(4,128)(2,1)S(1)} %get-tuple-element.13.rec_in, bf16[4,64,2304]{2,1,0:T(8,128)(2,1)S(1)} %get-tuple-element.14.dg_in, ...), custom_call_target="tpu_custom_call" | custom-call | tf_op jit(solution)/shard_map/emit/pallas_call | solution.py:392
